TPU v7x, 32 devices: a whole 2x2x4 slice. The times are simulated.
32 devices in a mesh: groups: 2 (over y), coord: 8 (over z, x), ckpt: 2 (over core).
Axes of the slice: x: 2, y: 2, z: 4, core: 2. Of those that a mesh axis runs over, the one named last changes fastest.
Arguments:
- projection_input: bfloat16 [2, 2, 384, 4096], P('ckpt', 'groups', None, 'coord'), parts along dimension 1, may hold values from -6 to 6
- gate_output_gradient: bfloat16 [2, 2, 14336, 384], P('ckpt', 'groups', 'coord'), parts along dimension 1, may hold values from -0.59765625 to 0.59765625
- up_output_gradient: bfloat16 [2, 2, 14336, 384], P('ckpt', 'groups', 'coord'), parts along dimension 1, may hold values from -0.59765625 to 0.59765625
- hidden: bfloat16 [2, 2, 14336, 384], P('ckpt', 'groups', 'coord'), parts along dimension 1, may hold values from -6 to 6
- down_output_gradient: bfloat16 [2, 2, 384, 4096], P('ckpt', 'groups', None, 'coord'), parts along dimension 1, may hold values from -0.59765625 to 0.59765625
- gate_adapter_first: bfloat16 [2, 4096, 128], P('ckpt', 'coord'), may hold values from -0.09375 to 0.09375
- gate_adapter_second: bfloat16 [2, 14336, 128], P('ckpt', 'coord'), may hold values from -0.5 to 0.5
- up_adapter_first: bfloat16 [2, 4096, 128], P('ckpt', 'coord'), may hold values from -0.09375 to 0.09375
- up_adapter_second: bfloat16 [2, 14336, 128], P('ckpt', 'coord'), may hold values from -0.5 to 0.5
- down_adapter_first: bfloat16 [2, 14336, 128], P('ckpt', 'coord'), may hold values from -0.046875 to 0.046875
- down_adapter_second: bfloat16 [2, 4096, 128], P('ckpt', 'coord'), may hold values from -0.5 to 0.5
- random_sign_flags: int32 [16777216], P(('coord', 'ckpt')), may hold values 0 or 1
- sampled_coordinate_index: int32 [8192], replicated, may hold values from 0 to 16777215
Outputs:
- features: float32 [2, 8192], P('groups'), parts along dimension 0
There are 2 independent parts, one for each index of `groups`. A program takes and returns all parts, laid end to end along the dimension named above; an argument that names none is the same for every part. Nothing has to cross between parts.
All inputs are finite; a program needn't handle non-finite values. No bound on the sum of `random_sign_flags` on one device may be relied on, other than what follows from the above.
Results may differ from a plain program's by a relative error of at most 0.0031.
Values may be sent and summed in bfloat16 or wider, within the bound.
A program may use at most 64 MiB of HBM per device.

v0:
```python
import jax
import jax.numpy as jnp
from jax import lax
from jax.sharding import PartitionSpec as P

HAD = 16777216
adapter_scale = 2.0


def partner_2(value, axis, apart):
    mask = 2**apart
    pairs = [(source, source ^ mask) for source in range(lax.axis_size(axis))]
    return lax.ppermute(value, axis, pairs)


def walsh_table(degree):
    positions = lax.iota(jnp.int32, degree)
    parity = jnp.zeros((degree, degree), jnp.int32)
    for bit_level in range(degree.bit_length() - 1):
        parity = parity + (positions[:, None] >> bit_level & 1) * (
            positions[None, :] >> bit_level & 1
        )
    return (1 - 2 * (parity % 2)).astype(jnp.float32)


def local_walsh(signed):
    prompts = signed.shape[0]
    count = signed.shape[1]
    inner_len = min(256, count)
    outer_len = count // inner_len
    tiling = signed.reshape(prompts, outer_len, inner_len)
    tiling = jnp.einsum(
        "eoi,ji->eoj", tiling, walsh_table(inner_len), precision=lax.Precision.HIGHEST
    )
    tiling = jnp.einsum(
        "eoi,po->epi", tiling, walsh_table(outer_len), precision=lax.Precision.HIGHEST
    )
    return tiling.reshape(prompts, count)


def matrix_product(form, left, right):
    return jnp.einsum(form, left, right, preferred_element_type=jnp.float32)


def shards(
    projection_input,
    gate_output_gradient,
    up_output_gradient,
    hidden,
    down_output_gradient,
    gate_adapter_first,
    gate_adapter_second,
    up_adapter_first,
    up_adapter_second,
    down_adapter_first,
    down_adapter_second,
    random_sign_flags,
    sampled_coordinate_index,
):
    input_tensors = projection_input[0]
    gate_cotangent_value = gate_output_gradient[0]
    up_cotangent_value = up_output_gradient[0]
    hidden_input_rows = hidden[0]
    output_cotangent_value = down_output_gradient[0]
    coord_count = lax.axis_size("coord")
    partials = (
        matrix_product("nuj,jx->nux", input_tensors, gate_adapter_first[0]),
        matrix_product("nuj,jx->nux", input_tensors, up_adapter_first[0]),
        matrix_product("udo,da->uoa", hidden_input_rows, down_adapter_first[0]),
        matrix_product("udo,da->uoa", gate_cotangent_value, gate_adapter_second[0]),
        matrix_product("udo,da->uoa", up_cotangent_value, up_adapter_second[0]),
        matrix_product("nuj,jx->nux", output_cotangent_value, down_adapter_second[0]),
    )
    summed = lax.psum(
        (partials[0], partials[1], partials[2], partials[3], partials[4], partials[5]), "coord"
    )
    (
        gate_forward_pass,
        up_forward_pass,
        down_forward_pass,
        gate_backward_pass,
        up_backward_pass,
        down_backward_pass,
    ) = [part.astype(jnp.bfloat16) for part in summed]
    prompts = input_tensors.shape[0]
    adapter_rank_value = gate_adapter_first.shape[2]
    local_len = random_sign_flags.shape[0]
    pieces = [
        adapter_scale * matrix_product("ktv,ktj->kvj", input_tensors, gate_backward_pass),
        adapter_scale * matrix_product("ktv,ktj->kvj", input_tensors, up_backward_pass),
        adapter_scale * matrix_product("ktv,ktj->kvj", output_cotangent_value, down_forward_pass),
        adapter_scale * matrix_product("jpx,jxg->jpg", gate_cotangent_value, gate_forward_pass),
        adapter_scale * matrix_product("jpx,jxg->jpg", up_cotangent_value, up_forward_pass),
        adapter_scale * matrix_product("jpx,jxg->jpg", hidden_input_rows, down_backward_pass),
    ]
    filled = 3 * input_tensors.shape[2] + 3 * gate_cotangent_value.shape[1]
    pieces.append(
        jnp.zeros(
            (prompts, local_len // adapter_rank_value - filled, adapter_rank_value), jnp.float32
        )
    )
    gradient = jnp.concatenate(pieces, axis=1).reshape(prompts, local_len)
    signed = gradient * (1.0 - 2.0 * random_sign_flags.astype(jnp.float32))[None, :]
    spectrum = local_walsh(signed)
    my_coord = lax.axis_index("coord")
    ensemble_member = lax.axis_index("ckpt")
    piece_len = local_len // coord_count
    table = walsh_table(coord_count)
    mixed_data = jnp.einsum(
        "ecr,gc->egr",
        lax.all_to_all(
            spectrum.reshape(prompts, coord_count, piece_len),
            "coord",
            split_axis=1,
            concat_axis=1,
            tiled=True,
        ),
        table,
        precision=lax.Precision.HIGHEST,
    ).reshape(prompts, local_len)
    partner = partner_2(mixed_data, "ckpt", 0)
    mixed_data = jnp.where(ensemble_member == 0, mixed_data + partner, partner - mixed_data)
    group_pos = sampled_coordinate_index // (2 * local_len)
    half_pos = sampled_coordinate_index // local_len % 2
    offset = sampled_coordinate_index % local_len
    owner_pos = offset // piece_len
    flat_pos = group_pos * piece_len + offset % piece_len
    weight = jnp.where((owner_pos == my_coord) & (half_pos == ensemble_member), 1.0, 0.0)
    chosen = jnp.take(mixed_data, flat_pos, axis=1)
    contrib = chosen * weight[None, :].astype(jnp.float32) * float(HAD) ** (-0.5)
    return lax.psum(contrib, ("coord", "ckpt"))


def solution(mesh):
    in_specs = (
        P("ckpt", "groups", None, "coord"),
        P("ckpt", "groups", "coord", None),
        P("ckpt", "groups", "coord", None),
        P("ckpt", "groups", "coord", None),
        P("ckpt", "groups", None, "coord"),
        P("ckpt", "coord", None),
        P("ckpt", "coord", None),
        P("ckpt", "coord", None),
        P("ckpt", "coord", None),
        P("ckpt", "coord", None),
        P("ckpt", "coord", None),
        P(("coord", "ckpt")),
        P(),
    )
    out_specs = P("groups", None)
    return jax.shard_map(shards, mesh=mesh, in_specs=in_specs, out_specs=out_specs, check_vma=False)
```

profile of v0, /device:TPU:0, one launch (start us, length us, event | category | flops | bytes accessed | tf_op | source)
XLA Modules:
  0.0 560.0 jit_solution(11059886902752881437)
XLA Ops:
  0.0 0.0 copy-start
  0.0 0.0 copy-start.7
  0.0 0.6 shift-right-arithmetic_and_fusion.12
  0.6 0.6 shift-right-arithmetic_and_fusion.14
  1.2 0.5 shift-right-arithmetic_and_fusion.16
  1.7 0.6 shift-right-arithmetic_and_fusion.18
  2.3 0.6 shift-right-arithmetic_and_fusion
  2.9 0.6 shift-right-arithmetic_and_fusion.2
  3.5 0.6 shift-right-arithmetic_and_fusion.4
  4.2 0.6 shift-right-arithmetic_and_fusion.6
  4.8 0.6 shift-right-arithmetic_and_fusion.8
  5.4 0.6 shift-right-arithmetic_and_fusion.10
  6.0 2.0 convolution_bitcast_fusion.1
  7.9 2.0 convolution_bitcast_fusion.2
  9.9 1.9 convolution_bitcast_fusion.3
  11.9 0.0 copy-done
  11.9 2.3 fusion.59
  14.2 0.0 copy-done.1
  14.2 0.0 copy-done.6
  14.2 1.2 fusion.62
  15.4 0.0 copy-done.2
  15.4 0.0 copy-done.7
  15.4 1.3 fusion.65
  16.7 76.4 %all-reduce.2 = (bf16[1,384,128]{2,1,0:T(8,128)(2,1)}, bf16[1,384,128]{2,1,0:T(8,128)(2,1)}, bf16[1,384,128]{2,1,0:T(8,128)(2,1)}, bf16[1,384,128]{2,1,0:T(8,128...) all-reduce(f32[1,384,128]{2,1,0:T(8,128)} %fusion.59, ...), channel_id=1, replica_groups=mesh['groups'=2,'coord'=8,'ckpt'=2] {'coord'}, use_global_device_ids=true, to_apply=%region_0.0 | all-reduce | flops 294912 | bytes 1769472 | tf_op jit(solution)/shard_map/psum | solution.py:74
  93.1 0.0 copy-done.4
  93.1 2.0 fusion.58
  95.1 1.9 fusion.56
  96.9 0.0 copy-done.5
  96.9 1.9 fusion.54
  98.8 2.5 fusion.39
  101.3 0.0 copy-done.10
  101.3 1.5 fusion.41
  102.7 0.0 copy-done.3
  102.8 0.0 copy-done.9
  102.8 1.5 fusion.43
  104.3 0.9 broadcast_dynamic-update-slice_fusion
  105.2 5.7 %copy.15 = f32[1,8192,128]{2,1,0:T(8,128)} copy(f32[1,8192,128]{1,2,0:T(8,128)} %broadcast_dynamic-update-slice_fusion) | data formatting | bytes 8388608 | tf_op jit(solution)/shard_map/concatenate | solution.py:102
  110.9 6.0 %bitcast_multiply_fusion = f32[1048576]{0:T(1024)} fusion(f32[1,8192,128]{2,1,0:T(8,128)} %copy.15, s32[1048576]{0:T(1024)} %param.24), kind=kLoop, calls=%fused_computation.43 | loop fusion | flops 4194304 | bytes 12582912 | tf_op jit(solution)/shard_map/mul | solution.py:103
  116.9 0.0 copy-start.26
  116.9 0.0 copy-start.27
  116.9 0.0 copy-start.28
  116.9 0.0 copy-start.29
  116.9 5.2 reshape.436
  122.1 0.0 copy-done.22
  122.1 0.0 copy-done.23
  122.1 0.0 copy-done.24
  122.2 0.0 copy-done.25
  122.2 0.0 copy-done.26
  122.2 0.0 copy-start.11
  122.3 6.0 %fusion.81 = f32[4096,256]{1,0:T(8,128)S(1)} fusion(f32[4096,256]{1,0:T(8,128)} %reshape.436, s32[256]{0:T(256)S(1)} %copy-done.22, s32[256]{0:T(256)S(1)} %copy-done.23, s32[256]{0:T(256)S(1)} %copy-done.24, s32[256]{0:T(256)S(1)} %copy-done.25, s32[256]{0:T(256)S(1)} %copy-done.26, s32[256]{0:T(256)S(1)} %copy-done.27, s32[256]{0:T(256)S(1)} %copy-done.28, ...), kind=kOutput, calls=%fused_computation.94 | convolution fusion | flops 3223126016 | bytes 8396800 | tf_op jit(solution)/shard_map/eoi,ji->eoj/dot_general | solution.py:32
  128.5 149.6 %fusion.4 = f32[4096,256]{1,0:T(8,128)} fusion(f32[4096,256]{1,0:T(8,128)S(1)} %fusion.81, s32[4096]{0:T(1024)S(1)} %get-tuple-element.19, s32[4096]{0:T(1024)S(1)} %copy-done.11, s32[4096]{0:T(1024)S(1)} %copy-done.12, s32[4096]{0:T(1024)S(1)} %copy-done.13, s32[4096]{0:T(1024)S(1)} %copy-done.14, s32[4096]{0:T(1024)S(1)} %copy-done.15, ...), kind=kOutput, calls=%fused_computation.9 | convolution fusion | flops 52160364544 | bytes 8585216 | tf_op jit(solution)/shard_map/eoi,po->epi/dot_general | solution.py:35
  278.1 8.4 %transpose.90 = f32[1,8,131072]{2,0,1:T(1,128)} reshape(f32[4096,256]{1,0:T(8,128)} %fusion.4) | data formatting | bytes 8388608 | tf_op jit(solution)/shard_map/reshape;reshape;eoi,po->epi/transpose | solution.py:112
  286.5 4.6 all-to-all-start
  291.1 83.1 %all-to-all-done = f32[1,8,131072]{2,0,1:T(1,128)} async-done(((f32[1,8,131072]{2,0,1:T(1,128)}), f32[1,8,131072]{2,0,1:T(1,128)}, u32[]{:S(2)}, u32[]{:S(2)}) %all-to-all-start) | async-done | bytes 4194336 | tf_op jit(solution)/shard_map/all_to_all | solution.py:111
  374.1 8.0 %convolution_bitcast_fusion = f32[1,1,8,131072]{3,2,1,0:T(8,128)S(1)} fusion(f32[1,8,131072]{2,0,1:T(1,128)} %all-to-all-done, s32[8]{0:T(128)S(1)} %get-tuple-element.31, s32[8]{0:T(128)S(1)} %get-tuple-element.32, s32[8]{0:T(128)S(1)} %shift-right-arithmetic_and_fusion.22), kind=kOutput, calls=%fused_computation.1 | convolution fusion | flops 100664512 | bytes 8388704 | tf_op jit(solution)/shard_map/ecr,gc->egr/dot_general | solution.py:109
  382.2 0.0 copy-start.8
  382.2 6.3 %copy.18 = f32[1,1,8,131072]{3,1,2,0:T(1,128)} copy(f32[1,1,8,131072]{3,2,1,0:T(8,128)S(1)} %convolution_bitcast_fusion) | data formatting | bytes 8388608
  388.5 0.0 collective-permute-start
  388.5 0.1 fusion.130
  388.6 7.4 %collective-permute-done = f32[1,1048576]{1,0:T(1,128)} collective-permute-done((f32[1,1048576]{1,0:T(1,128)}, f32[1,1048576]{1,0:T(1,128)}, u32[]{:S(2)}, u32[]{:S(2)}) %collective-permute-start) | collective-permute-done | bytes 4194336 | tf_op jit(solution)/shard_map/ppermute | solution.py:13
  396.0 7.2 %broadcast_select_fusion = f32[1,1048576]{1,0:T(1,128)} fusion(pred[]{:T(512)S(6)} %eq.25, f32[1,1048576]{1,0:T(1,128)} %collective-permute-done, f32[1,1048576]{1,0:T(1,128)} %bitcast.135), kind=kLoop, calls=%fused_computation.40 | loop fusion | flops 3145728 | bytes 12582913 | tf_op jit(solution)/shard_map/jit(_where)/select_n | solution.py:122
  403.2 96.3 %gather_fusion = f32[8192]{0:T(1024)S(1)} fusion(f32[1048576]{0:T(1024)} %bitcast.133, s32[8192]{0:T(1024)S(1)} %fusion.130), kind=kCustom, calls=%fused_computation | custom fusion | bytes 98304 | tf_op jit(solution)/shard_map/jit(_take)/gather | solution.py:129
  499.5 0.1 multiply_multiply_fusion
  499.6 60.0 %psum.55 = f32[1,8192]{1,0:T(1,128)} all-reduce(f32[1,8192]{1,0:T(1,128)S(1)} %bitcast.136), channel_id=1, replica_groups=mesh['groups'=2,'coord'=8,'ckpt'=2] {'coord','ckpt'}, use_global_device_ids=true, to_apply=%region_6.7 | all-reduce | flops 8192 | bytes 65536 | tf_op jit(solution)/shard_map/psum | solution.py:131
  (39 shorter events, 0.1 us)
Async XLA Ops:
  0.0 11.9 %copy-start = (bf16[1,1,1792,384]{3,2,1,0:T(8,128)(2,1)S(1)}, bf16[1,1,1792,384]{3,2,1,0:T(8,128)(2,1)}, u32[]{:S(2)}) copy-start(bf16[1,1,1792,384]{3,2,1,0:T(8,128)(2,1)} %param.14) | copy-start | bytes 4128772
  0.0 14.2 %copy-start.1 = (bf16[1,1,1792,384]{3,2,1,0:T(8,128)(2,1)S(1)}, bf16[1,1,1792,384]{3,2,1,0:T(8,128)(2,1)}, u32[]{:S(2)}) copy-start(bf16[1,1,1792,384]{3,2,1,0:T(8,128)(2,1)} %param.15) | copy-start | bytes 4128772
  0.0 14.2 %copy-start.6 = (bf16[1,1792,128]{2,1,0:T(8,128)(2,1)S(1)}, bf16[1,1792,128]{2,1,0:T(8,128)(2,1)}, u32[]{:S(2)}) copy-start(bf16[1,1792,128]{2,1,0:T(8,128)(2,1)} %param.21) | copy-start | bytes 1376260
  0.0 15.4 %copy-start.2 = (bf16[1,1,1792,384]{3,2,1,0:T(8,128)(2,1)S(1)}, bf16[1,1,1792,384]{3,2,1,0:T(8,128)(2,1)}, u32[]{:S(2)}) copy-start(bf16[1,1,1792,384]{3,2,1,0:T(8,128)(2,1)} %param.16) | copy-start | bytes 4128772
  0.0 15.4 %copy-start.7 = (bf16[1,1792,128]{2,1,0:T(8,128)(2,1)S(1)}, bf16[1,1792,128]{2,1,0:T(8,128)(2,1)}, u32[]{:S(2)}) copy-start(bf16[1,1792,128]{2,1,0:T(8,128)(2,1)} %param.22) | copy-start | bytes 1376260
  11.9 81.2 %copy-start.4 = (bf16[1,1,384,512]{3,2,1,0:T(8,128)(2,1)S(1)}, bf16[1,1,384,512]{3,2,1,0:T(8,128)(2,1)}, u32[]{:S(2)}) copy-start(bf16[1,1,384,512]{3,2,1,0:T(8,128)(2,1)} %param.13) | copy-start | bytes 1179652
  14.2 82.7 %copy-start.5 = (bf16[1,1,384,512]{3,2,1,0:T(8,128)(2,1)S(1)}, bf16[1,1,384,512]{3,2,1,0:T(8,128)(2,1)}, u32[]{:S(2)}) copy-start(bf16[1,1,384,512]{3,2,1,0:T(8,128)(2,1)} %param.17) | copy-start | bytes 1179652
  93.1 8.2 %copy-start.10 = (bf16[1,384,128]{2,1,0:T(8,128)(2,1)S(1)}, bf16[1,384,128]{2,1,0:T(8,128)(2,1)}, u32[]{:S(2)}) copy-start(bf16[1,384,128]{2,1,0:T(8,128)(2,1)} %get-tuple-element.9) | copy-start | bytes 294916
  93.1 9.7 %copy-start.3 = (bf16[1,1,1792,384]{3,2,1,0:T(8,128)(2,1)S(1)}, bf16[1,1,1792,384]{3,2,1,0:T(8,128)(2,1)}, u32[]{:S(2)}) copy-start(bf16[1,1,1792,384]{3,2,1,0:T(8,128)(2,1)} %param.16) | copy-start | bytes 4128772
  93.1 9.7 %copy-start.9 = (bf16[1,384,128]{2,1,0:T(8,128)(2,1)S(1)}, bf16[1,384,128]{2,1,0:T(8,128)(2,1)}, u32[]{:S(2)}) copy-start(bf16[1,384,128]{2,1,0:T(8,128)(2,1)} %get-tuple-element.10) | copy-start | bytes 294916
  116.9 5.3 copy-start.22
  116.9 5.3 copy-start.23
  116.9 5.3 copy-start.24
  116.9 5.3 copy-start.25
  116.9 5.3 copy-start.26
  116.9 5.3 copy-start.27
  116.9 5.3 copy-start.28
  116.9 5.3 copy-start.29
  122.2 6.2 %copy-start.11 = (s32[4096]{0:T(1024)S(1)}, s32[4096]{0:T(1024)}, u32[]{:S(2)}) copy-start(s32[4096]{0:T(1024)} %get-tuple-element.20) | copy-start | bytes 49156
  122.2 6.2 %copy-start.12 = (s32[4096]{0:T(1024)S(1)}, s32[4096]{0:T(1024)}, u32[]{:S(2)}) copy-start(s32[4096]{0:T(1024)} %get-tuple-element.21) | copy-start | bytes 49156
  122.2 6.2 %copy-start.13 = (s32[4096]{0:T(1024)S(1)}, s32[4096]{0:T(1024)}, u32[]{:S(2)}) copy-start(s32[4096]{0:T(1024)} %get-tuple-element.22) | copy-start | bytes 49156
  122.2 6.2 %copy-start.14 = (s32[4096]{0:T(1024)S(1)}, s32[4096]{0:T(1024)}, u32[]{:S(2)}) copy-start(s32[4096]{0:T(1024)} %get-tuple-element.23) | copy-start | bytes 49156
  122.2 6.2 %copy-start.15 = (s32[4096]{0:T(1024)S(1)}, s32[4096]{0:T(1024)}, u32[]{:S(2)}) copy-start(s32[4096]{0:T(1024)} %get-tuple-element.24) | copy-start | bytes 49156
  122.3 6.2 %copy-start.16 = (s32[4096]{0:T(1024)S(1)}, s32[4096]{0:T(1024)}, u32[]{:S(2)}) copy-start(s32[4096]{0:T(1024)} %get-tuple-element.25) | copy-start | bytes 49156
  122.3 6.2 %copy-start.17 = (s32[4096]{0:T(1024)S(1)}, s32[4096]{0:T(1024)}, u32[]{:S(2)}) copy-start(s32[4096]{0:T(1024)} %get-tuple-element.26) | copy-start | bytes 49156
  122.3 6.2 %copy-start.18 = (s32[4096]{0:T(1024)S(1)}, s32[4096]{0:T(1024)}, u32[]{:S(2)}) copy-start(s32[4096]{0:T(1024)} %get-tuple-element.27) | copy-start | bytes 49156
  122.3 6.2 %copy-start.19 = (s32[4096]{0:T(1024)S(1)}, s32[4096]{0:T(1024)}, u32[]{:S(2)}) copy-start(s32[4096]{0:T(1024)} %get-tuple-element.28) | copy-start | bytes 49156
  122.3 6.2 %copy-start.20 = (s32[4096]{0:T(1024)S(1)}, s32[4096]{0:T(1024)}, u32[]{:S(2)}) copy-start(s32[4096]{0:T(1024)} %get-tuple-element.29) | copy-start | bytes 49156
  122.3 6.2 %copy-start.21 = (s32[4096]{0:T(1024)S(1)}, s32[4096]{0:T(1024)}, u32[]{:S(2)}) copy-start(s32[4096]{0:T(1024)} %get-tuple-element.30) | copy-start | bytes 49156
  286.5 87.6 %all-to-all-start = ((f32[1,8,131072]{2,0,1:T(1,128)}), f32[1,8,131072]{2,0,1:T(1,128)}, u32[]{:S(2)}, u32[]{:S(2)}) async-start(f32[1,8,131072]{2,0,1:T(1,128)} %transpose.90), calls=%async_computation | async-start | bytes 8388608 | tf_op jit(solution)/shard_map/all_to_all | solution.py:111
  382.2 6.3 %copy-start.8 = (s32[8192]{0:T(1024)S(1)}, s32[8192]{0:T(1024)}, u32[]{:S(2)}) copy-start(s32[8192]{0:T(1024)} %param.25) | copy-start | bytes 98308
  388.5 7.5 %collective-permute-start = (f32[1,1048576]{1,0:T(1,128)}, f32[1,1048576]{1,0:T(1,128)}, u32[]{:S(2)}, u32[]{:S(2)}) collective-permute-start(f32[1,1048576]{1,0:T(1,128)} %bitcast.134), channel_id=1, source_target_pairs={{0,1},{1,0},{2,3},{3,2},{4,5},{5,4},{6,7},{7,6},{8,9},{9,8},{10,11... | collective-permute-start | bytes 12582920 | tf_op jit(solution)/shard_map/ppermute | solution.py:13
where the time goes:
time: 571 us; the launch traced here: 560 us
  matrix products  186 us (33%)
  blocking collectives  136 us (24%)
  local copies, waits for them, and re-layouts  123 us (22%)
  waiting for transfers between devices  90.5 us (16%)
  other arithmetic  19.3 us (3%)
    dot_general x1, matrix products, local_walsh(): jnp.einsum('eoi,po->epi', tiling, walsh_table(outer_len), precision=lax.P...  150 us
    gather x1, local copies, waits for them, and re-layouts, shards(): chosen = jnp.take(mixed_data, flat_pos, axis=1)  96.3 us
    all_to_all x1, waiting for transfers between devices, shards(): lax.all_to_all(spectrum.reshape(prompts, coord_count, piece_len), 'coord'...  83.1 us
    psum x1, blocking collectives, shards(): lax.psum((partials[0], partials[1], partials[2], partials[3], partials[4]...  76.4 us
    psum x1, blocking collectives, shards(): return lax.psum(contrib, ('coord', 'ckpt'))  60 us
    dot_general x12, matrix products, matrix_product(): return jnp.einsum(form, left, right, preferred_element_type=jnp.float32)  21.9 us
  transfers between devices with their start and end apart: 2, of which 2 were waited for; matrix products, arithmetic and copies ran while one was open for 0% of the time, Pallas kernels for 0%

commit v1 on v0

--- a/solution.py
+++ b/solution.py
@@ -108,12 +108,20 @@
     table = walsh_table(coord_count)
     mixed_data = jnp.einsum(
         "ecr,gc->egr",
-        lax.all_to_all(
-            spectrum.reshape(prompts, coord_count, piece_len),
-            "coord",
-            split_axis=1,
-            concat_axis=1,
-            tiled=True,
+        jnp.concatenate(
+            lax.all_to_all(
+                jnp.stack(
+                    jnp.split(
+                        spectrum.reshape(prompts, coord_count, piece_len),
+                        lax.axis_size("coord"),
+                        axis=1,
+                    )
+                ),
+                "coord",
+                0,
+                0,
+            ),
+            axis=1,
         ),
         table,
         precision=lax.Precision.HIGHEST,

time: 571 us -> 594 us (1.040)
  local copies, waits for them, and re-layouts: 123 us -> 147 us
    unnamed x61 -> x70, local copies, waits for them, and re-layouts: 6.42 us -> 30.4 us
where the time goes in v1:
time: 594 us; the launch traced here: 583 us
  matrix products  184 us (31%)
  local copies, waits for them, and re-layouts  147 us (25%)
  blocking collectives  137 us (23%)
  waiting for transfers between devices  90.2 us (15%)
  other arithmetic  19.4 us (3%)
    dot_general x1, matrix products, local_walsh(): jnp.einsum('eoi,po->epi', tiling, walsh_table(outer_len), precision=lax.P...  148 us
    gather x1, local copies, waits for them, and re-layouts, shards(): chosen = jnp.take(mixed_data, flat_pos, axis=1)  96.3 us
    all_to_all x1, waiting for transfers between devices, shards(): lax.all_to_all(jnp.stack(jnp.split(spectrum.reshape(prompts, coord_count,...  82.8 us
    psum x1, blocking collectives, shards(): lax.psum((partials[0], partials[1], partials[2], partials[3], partials[4]...  76.6 us
    psum x1, blocking collectives, shards(): return lax.psum(contrib, ('coord', 'ckpt'))  60 us
    unnamed x70, local copies, waits for them, and re-layouts  30.4 us
    dot_general x12, matrix products, matrix_product(): return jnp.einsum(form, left, right, preferred_element_type=jnp.float32)  22 us
  transfers between devices with their start and end apart: 2, of which 2 were waited for; matrix products, arithmetic and copies ran while one was open for 0% of the time, Pallas kernels for 0%

profile of v1, /device:TPU:0, one launch (start us, length us, event | category | flops | bytes accessed | tf_op | source)
XLA Modules:
  0.0 582.5 jit_solution(746780758157271625)
XLA Ops:
  0.0 0.0 copy-start
  0.0 0.0 copy-start.8
  0.0 0.6 shift-right-arithmetic_and_fusion.12
  0.6 0.6 shift-right-arithmetic_and_fusion.14
  1.2 0.6 shift-right-arithmetic_and_fusion.16
  1.8 0.5 shift-right-arithmetic_and_fusion.18
  2.3 0.6 shift-right-arithmetic_and_fusion
  2.9 0.6 shift-right-arithmetic_and_fusion.2
  3.6 0.6 shift-right-arithmetic_and_fusion.4
  4.2 0.6 shift-right-arithmetic_and_fusion.6
  4.8 0.6 shift-right-arithmetic_and_fusion.8
  5.4 0.6 shift-right-arithmetic_and_fusion.10
  6.0 2.0 convolution_bitcast_fusion.1
  8.0 2.0 convolution_bitcast_fusion.2
  10.0 2.0 convolution_bitcast_fusion.3
  11.9 0.0 copy-done
  11.9 2.3 fusion.59
  14.2 0.0 copy-done.2
  14.3 0.0 copy-done.7
  14.3 1.2 fusion.62
  15.5 0.0 copy-done.3
  15.5 0.0 copy-done.8
  15.5 1.3 fusion.65
  16.8 76.6 %all-reduce.2 = (bf16[1,384,128]{2,1,0:T(8,128)(2,1)}, bf16[1,384,128]{2,1,0:T(8,128)(2,1)}, bf16[1,384,128]{2,1,0:T(8,128)(2,1)}, bf16[1,384,128]{2,1,0:T(8,128...) all-reduce(f32[1,384,128]{2,1,0:T(8,128)} %fusion.59, ...), channel_id=1, replica_groups=mesh['groups'=2,'coord'=8,'ckpt'=2] {'coord'}, use_global_device_ids=true, to_apply=%region_0.0 | all-reduce | flops 294912 | bytes 1769472 | tf_op jit(solution)/shard_map/psum | solution.py:74
  93.4 0.0 copy-done.5
  93.4 2.0 fusion.58
  95.3 1.9 fusion.56
  97.2 0.0 copy-done.6
  97.2 1.9 fusion.54
  99.1 2.4 fusion.39
  101.6 0.0 copy-done.11
  101.6 1.5 fusion.41
  103.1 0.0 copy-done.4
  103.1 0.0 copy-done.10
  103.1 1.6 fusion.43
  104.7 0.9 broadcast_dynamic-update-slice_fusion
  105.6 5.7 copy.14
  111.3 6.0 %bitcast_multiply_fusion = f32[1048576]{0:T(1024)} fusion(f32[1,8192,128]{2,1,0:T(8,128)} %copy.14, s32[1048576]{0:T(1024)} %param.24), kind=kLoop, calls=%fused_computation.43 | loop fusion | flops 4194304 | bytes 12582912 | tf_op jit(solution)/shard_map/mul | solution.py:103
  117.3 0.0 copy-start.27
  117.3 5.2 reshape.438
  122.6 0.0 copy-start.12
  122.7 6.1 %fusion.89 = f32[4096,256]{1,0:T(8,128)S(1)} fusion(f32[4096,256]{1,0:T(8,128)} %reshape.438, s32[256]{0:T(256)S(1)} %copy-done.23, s32[256]{0:T(256)S(1)} %copy-done.24, s32[256]{0:T(256)S(1)} %copy-done.25, s32[256]{0:T(256)S(1)} %copy-done.26, s32[256]{0:T(256)S(1)} %copy-done.27, s32[256]{0:T(256)S(1)} %copy-done.28, s32[256]{0:T(256)S(1)} %copy-done.29, ...), kind=kOutput, calls=%fused_computation.110 | convolution fusion | flops 3223126016 | bytes 8396800 | tf_op jit(solution)/shard_map/eoi,ji->eoj/dot_general | solution.py:32
  128.9 148.0 %fusion.4 = f32[4096,256]{1,0:T(8,128)} fusion(f32[4096,256]{1,0:T(8,128)S(1)} %fusion.89, s32[4096]{0:T(1024)S(1)} %get-tuple-element.19, s32[4096]{0:T(1024)S(1)} %copy-done.12, s32[4096]{0:T(1024)S(1)} %copy-done.13, s32[4096]{0:T(1024)S(1)} %copy-done.14, s32[4096]{0:T(1024)S(1)} %copy-done.15, s32[4096]{0:T(1024)S(1)} %copy-done.16, ...), kind=kOutput, calls=%fused_computation.9 | convolution fusion | flops 52160364544 | bytes 8585216 | tf_op jit(solution)/shard_map/eoi,po->epi/dot_general | solution.py:35
  276.9 4.9 transpose.82
  281.8 3.3 fusion.75
  285.1 3.5 fusion.74
  288.5 3.4 fusion.73
  292.0 3.4 fusion.72
  295.4 3.4 fusion.71
  298.9 3.4 fusion.70
  302.3 3.5 fusion.69
  305.8 3.5 fusion.68
  309.2 4.6 all-to-all-start
  313.8 82.8 %all-to-all-done = f32[8,1,1,131072]{3,2,1,0:T(1,128)} async-done(((f32[8,1,1,131072]{3,2,1,0:T(1,128)}), f32[8,1,1,131072]{3,2,1,0:T(1,128)}, u32[]{:S(2)}, u32[]{:S(2)}) %all-to-all-start) | async-done | bytes 4194336 | tf_op jit(solution)/shard_map/all_to_all | solution.py:112
  396.6 8.0 %convolution_bitcast_fusion = f32[1,1,8,131072]{3,2,1,0:T(8,128)S(1)} fusion(f32[8,1,1,131072]{3,2,1,0:T(1,128)} %all-to-all-done, s32[8]{0:T(128)S(1)} %get-tuple-element.31, s32[8]{0:T(128)S(1)} %get-tuple-element.32, s32[8]{0:T(128)S(1)} %shift-right-arithmetic_and_fusion.22), kind=kOutput, calls=%fused_computation.1 | convolution fusion | flops 100664512 | bytes 8388704 | tf_op jit(solution)/shard_map/ecr,gc->egr/dot_general | solution.py:109
  404.7 0.0 copy-start.9
  404.7 6.3 %copy.16 = f32[1,1,8,131072]{3,1,2,0:T(1,128)} copy(f32[1,1,8,131072]{3,2,1,0:T(8,128)S(1)} %convolution_bitcast_fusion) | data formatting | bytes 8388608
  411.0 0.0 collective-permute-start
  411.0 0.1 fusion.138
  411.0 7.4 %collective-permute-done = f32[1,1048576]{1,0:T(1,128)} collective-permute-done((f32[1,1048576]{1,0:T(1,128)}, f32[1,1048576]{1,0:T(1,128)}, u32[]{:S(2)}, u32[]{:S(2)}) %collective-permute-start) | collective-permute-done | bytes 4194336 | tf_op jit(solution)/shard_map/ppermute | solution.py:13
  418.5 7.2 %broadcast_select_fusion = f32[1,1048576]{1,0:T(1,128)} fusion(pred[]{:T(512)S(6)} %eq.25, f32[1,1048576]{1,0:T(1,128)} %collective-permute-done, f32[1,1048576]{1,0:T(1,128)} %bitcast.167), kind=kLoop, calls=%fused_computation.40 | loop fusion | flops 3145728 | bytes 12582913 | tf_op jit(solution)/shard_map/jit(_where)/select_n | solution.py:130
  425.7 96.3 %gather_fusion = f32[8192]{0:T(1024)S(1)} fusion(f32[1048576]{0:T(1024)} %bitcast.165, s32[8192]{0:T(1024)S(1)} %fusion.138), kind=kCustom, calls=%fused_computation | custom fusion | bytes 98304 | tf_op jit(solution)/shard_map/jit(_take)/gather | solution.py:137
  522.0 0.1 multiply_multiply_fusion
  522.1 60.0 %psum.55 = f32[1,8192]{1,0:T(1,128)} all-reduce(f32[1,8192]{1,0:T(1,128)S(1)} %bitcast.168), channel_id=1, replica_groups=mesh['groups'=2,'coord'=8,'ckpt'=2] {'coord','ckpt'}, use_global_device_ids=true, to_apply=%region_6.7 | all-reduce | flops 8192 | bytes 65536 | tf_op jit(solution)/shard_map/psum | solution.py:139
  (49 shorter events, 0.1 us)
Async XLA Ops:
  0.0 11.9 %copy-start = (bf16[1,1,1792,384]{3,2,1,0:T(8,128)(2,1)S(1)}, bf16[1,1,1792,384]{3,2,1,0:T(8,128)(2,1)}, u32[]{:S(2)}) copy-start(bf16[1,1,1792,384]{3,2,1,0:T(8,128)(2,1)} %param.14) | copy-start | bytes 4128772
  0.0 14.2 %copy-start.2 = (bf16[1,1,1792,384]{3,2,1,0:T(8,128)(2,1)S(1)}, bf16[1,1,1792,384]{3,2,1,0:T(8,128)(2,1)}, u32[]{:S(2)}) copy-start(bf16[1,1,1792,384]{3,2,1,0:T(8,128)(2,1)} %param.15) | copy-start | bytes 4128772
  0.0 14.2 %copy-start.7 = (bf16[1,1792,128]{2,1,0:T(8,128)(2,1)S(1)}, bf16[1,1792,128]{2,1,0:T(8,128)(2,1)}, u32[]{:S(2)}) copy-start(bf16[1,1792,128]{2,1,0:T(8,128)(2,1)} %param.21) | copy-start | bytes 1376260
  0.0 15.5 %copy-start.3 = (bf16[1,1,1792,384]{3,2,1,0:T(8,128)(2,1)S(1)}, bf16[1,1,1792,384]{3,2,1,0:T(8,128)(2,1)}, u32[]{:S(2)}) copy-start(bf16[1,1,1792,384]{3,2,1,0:T(8,128)(2,1)} %param.16) | copy-start | bytes 4128772
  0.0 15.5 %copy-start.8 = (bf16[1,1792,128]{2,1,0:T(8,128)(2,1)S(1)}, bf16[1,1792,128]{2,1,0:T(8,128)(2,1)}, u32[]{:S(2)}) copy-start(bf16[1,1792,128]{2,1,0:T(8,128)(2,1)} %param.22) | copy-start | bytes 1376260
  11.9 81.4 %copy-start.5 = (bf16[1,1,384,512]{3,2,1,0:T(8,128)(2,1)S(1)}, bf16[1,1,384,512]{3,2,1,0:T(8,128)(2,1)}, u32[]{:S(2)}) copy-start(bf16[1,1,384,512]{3,2,1,0:T(8,128)(2,1)} %param.13) | copy-start | bytes 1179652
  14.3 83.0 %copy-start.6 = (bf16[1,1,384,512]{3,2,1,0:T(8,128)(2,1)S(1)}, bf16[1,1,384,512]{3,2,1,0:T(8,128)(2,1)}, u32[]{:S(2)}) copy-start(bf16[1,1,384,512]{3,2,1,0:T(8,128)(2,1)} %param.17) | copy-start | bytes 1179652
  93.4 8.2 %copy-start.11 = (bf16[1,384,128]{2,1,0:T(8,128)(2,1)S(1)}, bf16[1,384,128]{2,1,0:T(8,128)(2,1)}, u32[]{:S(2)}) copy-start(bf16[1,384,128]{2,1,0:T(8,128)(2,1)} %get-tuple-element.9) | copy-start | bytes 294916
  93.4 9.7 %copy-start.4 = (bf16[1,1,1792,384]{3,2,1,0:T(8,128)(2,1)S(1)}, bf16[1,1,1792,384]{3,2,1,0:T(8,128)(2,1)}, u32[]{:S(2)}) copy-start(bf16[1,1,1792,384]{3,2,1,0:T(8,128)(2,1)} %param.16) | copy-start | bytes 4128772
  93.4 9.7 %copy-start.10 = (bf16[1,384,128]{2,1,0:T(8,128)(2,1)S(1)}, bf16[1,384,128]{2,1,0:T(8,128)(2,1)}, u32[]{:S(2)}) copy-start(bf16[1,384,128]{2,1,0:T(8,128)(2,1)} %get-tuple-element.10) | copy-start | bytes 294916
  117.3 5.3 copy-start.23
  117.3 5.3 copy-start.24
  117.3 5.3 copy-start.25
  117.3 5.3 copy-start.26
  117.3 5.3 copy-start.27
  117.3 5.3 copy-start.28
  117.3 5.3 copy-start.29
  117.3 5.3 copy-start.30
  122.6 6.2 %copy-start.12 = (s32[4096]{0:T(1024)S(1)}, s32[4096]{0:T(1024)}, u32[]{:S(2)}) copy-start(s32[4096]{0:T(1024)} %get-tuple-element.20) | copy-start | bytes 49156
  122.6 6.2 %copy-start.13 = (s32[4096]{0:T(1024)S(1)}, s32[4096]{0:T(1024)}, u32[]{:S(2)}) copy-start(s32[4096]{0:T(1024)} %get-tuple-element.21) | copy-start | bytes 49156
  122.7 6.2 %copy-start.14 = (s32[4096]{0:T(1024)S(1)}, s32[4096]{0:T(1024)}, u32[]{:S(2)}) copy-start(s32[4096]{0:T(1024)} %get-tuple-element.22) | copy-start | bytes 49156
  122.7 6.2 %copy-start.15 = (s32[4096]{0:T(1024)S(1)}, s32[4096]{0:T(1024)}, u32[]{:S(2)}) copy-start(s32[4096]{0:T(1024)} %get-tuple-element.23) | copy-start | bytes 49156
  122.7 6.2 %copy-start.16 = (s32[4096]{0:T(1024)S(1)}, s32[4096]{0:T(1024)}, u32[]{:S(2)}) copy-start(s32[4096]{0:T(1024)} %get-tuple-element.24) | copy-start | bytes 49156
  122.7 6.2 %copy-start.17 = (s32[4096]{0:T(1024)S(1)}, s32[4096]{0:T(1024)}, u32[]{:S(2)}) copy-start(s32[4096]{0:T(1024)} %get-tuple-element.25) | copy-start | bytes 49156
  122.7 6.2 %copy-start.18 = (s32[4096]{0:T(1024)S(1)}, s32[4096]{0:T(1024)}, u32[]{:S(2)}) copy-start(s32[4096]{0:T(1024)} %get-tuple-element.26) | copy-start | bytes 49156
  122.7 6.2 %copy-start.19 = (s32[4096]{0:T(1024)S(1)}, s32[4096]{0:T(1024)}, u32[]{:S(2)}) copy-start(s32[4096]{0:T(1024)} %get-tuple-element.27) | copy-start | bytes 49156
  122.7 6.2 %copy-start.20 = (s32[4096]{0:T(1024)S(1)}, s32[4096]{0:T(1024)}, u32[]{:S(2)}) copy-start(s32[4096]{0:T(1024)} %get-tuple-element.28) | copy-start | bytes 49156
  122.7 6.2 %copy-start.21 = (s32[4096]{0:T(1024)S(1)}, s32[4096]{0:T(1024)}, u32[]{:S(2)}) copy-start(s32[4096]{0:T(1024)} %get-tuple-element.29) | copy-start | bytes 49156
  122.7 6.2 %copy-start.22 = (s32[4096]{0:T(1024)S(1)}, s32[4096]{0:T(1024)}, u32[]{:S(2)}) copy-start(s32[4096]{0:T(1024)} %get-tuple-element.30) | copy-start | bytes 49156
  309.2 87.4 %all-to-all-start = ((f32[8,1,1,131072]{3,2,1,0:T(1,128)}), f32[8,1,1,131072]{3,2,1,0:T(1,128)}, u32[]{:S(2)}, u32[]{:S(2)}) async-start(f32[8,1,1,131072]{3,2,1,0:T(1,128)} %fusion.68), calls=%async_computation | async-start | bytes 8388608 | tf_op jit(solution)/shard_map/all_to_all | solution.py:112
  404.7 6.3 %copy-start.9 = (s32[8192]{0:T(1024)S(1)}, s32[8192]{0:T(1024)}, u32[]{:S(2)}) copy-start(s32[8192]{0:T(1024)} %param.25) | copy-start | bytes 98308
  411.0 7.5 %collective-permute-start = (f32[1,1048576]{1,0:T(1,128)}, f32[1,1048576]{1,0:T(1,128)}, u32[]{:S(2)}, u32[]{:S(2)}) collective-permute-start(f32[1,1048576]{1,0:T(1,128)} %bitcast.166), channel_id=1, source_target_pairs={{0,1},{1,0},{2,3},{3,2},{4,5},{5,4},{6,7},{7,6},{8,9},{9,8},{10,11... | collective-permute-start | bytes 12582920 | tf_op jit(solution)/shard_map/ppermute | solution.py:13
  425.7 156.5 %copy-start.1 = (bf16[1,1,1792,384]{3,2,1,0:T(8,128)(2,1)S(1)}, bf16[1,1,1792,384]{3,2,1,0:T(8,128)(2,1)}, u32[]{:S(2)}) copy-start(bf16[1,1,1792,384]{3,2,1,0:T(8,128)(2,1)} %param.14) | copy-start | bytes 4128772
